TPU v7x, 32 devices: a whole 2x2x4 slice. The times are simulated.
32 devices in a mesh: space: 8 (over z, y), slab: 4 (over x, core).
Axes of the slice: x: 2, y: 2, z: 4, core: 2. Of those that a mesh axis runs over, the one named last changes fastest.
Arguments:
- features: float32 [128, 8, 8, 512], P(('space', 'slab')), may hold values from -6 to 6
- live: int32 [32], P(('space', 'slab')), may hold values from 1 to 4, as said below
- rim_slots: int32 [32, 2], P(('space', 'slab')), may hold values from 0 to 3, as said below
- neighbours: int32 [128, 26], P(('space', 'slab')), may hold values from 0 to 12, as said below
- weights: float32 [4, 27, 4096], replicated, may hold values from -0.15625 to 0.15625
- biases: float32 [4, 64], replicated, may hold values from -3 to 3
Outputs:
- output: float32 [128, 8, 8, 512], P(('space', 'slab'))
Inputs may be any that keep to these rules, and one draw needn't show every extreme that they name: `live`: devices whose space indices differ by 8 / 2 (same slab index) hold at most 6 occupied bricks together; in every draw some pair holds exactly that and some device holds 4. `rim_slots`: every entry is below its device's live count. `neighbours`: entries below 4 are below the device's live count.
All inputs are finite; a program needn't handle non-finite values.
Results may differ from a plain program's by a relative error of at most 0.0003.
Values sent between devices are 32-bit elements; how exact they have to be, the bound alone decides.
A program may use at most 128 MiB of HBM per device.

v0:
```python
import functools

import jax
import jax.numpy as jnp
from jax import lax
from jax.experimental import pallas as pl
from jax.experimental.pallas import tpu as pltpu
from jax.sharding import PartitionSpec as P

MESH = pl.DeviceIdType.MESH
SIDE = 8


def direction_number(dx, dy, dz):
    index = 9 * (dx + 1) + 3 * (dy + 1) + (dz + 1)
    return index if index < 13 else index - 1


def layers_kernel(
    nsp, nsl, nbr, live, rim, feat, bias, w_hbm, out,
    cur, hid, own, offer, pad, cols, whi, wlo, wbuf, acc,
    wsem, ssem, rsem, *tabs,
):
    bricks = feat.shape[0]
    width = feat.shape[-1]
    ch = width // SIDE
    half = width // 2
    pair = 2 * ch
    ktile = half + pair
    kdy = 3 * ktile
    rims = offer.shape[1]
    convs = w_hbm.shape[0]
    sp = lax.axis_index("space")
    sl = lax.axis_index("slab")
    peers = (
        (sp > 0, (sp - 1, sl)),
        (sp < nsp - 1, (sp + 1, sl)),
        (sl > 0, (sp, sl - 1)),
        (sl < nsl - 1, (sp, sl + 1)),
    )

    barrier = pltpu.get_barrier_semaphore()
    for has, peer in peers:
        @pl.when(has)
        def _():
            pl.semaphore_signal(barrier, inc=1, device_id=peer, device_id_type=MESH)

    def weight_copy(k):
        return pltpu.make_async_copy(w_hbm.at[k], wbuf.at[k], wsem.at[k])

    for k in range(convs):
        weight_copy(k).start()

    def remote(k, d):
        first = bricks + rims * (d ^ 1)
        return pltpu.make_async_remote_copy(
            src_ref=offer.at[k],
            dst_ref=tabs[k].at[pl.ds(first, rims)],
            send_sem=ssem.at[k, d],
            recv_sem=rsem.at[k, d ^ 1],
            device_id=peers[d][1],
            device_id_type=MESH,
        )

    def mask_of(b):
        return jnp.where(b < live[0], 1.0, 0.0).astype(jnp.float32)

    low = lax.broadcasted_iota(jnp.int32, (SIDE, pair), 1) < ch
    low1 = lax.broadcasted_iota(jnp.int32, (1, pair), 1) < ch

    def take_faces(src, k):
        def one(b, carry):
            own[b, 0] = src[b, 0]
            own[b, 1] = src[b, SIDE - 1]
            for s, y in ((2, 0), (3, SIDE - 1)):
                for x in range(SIDE):
                    own[b, s, x:x + 1, :] = src[b, x, y:y + 1, :]
            for x in range(SIDE):
                at = (x % 4) * pair
                own[b, 4 + x // 4, :, at:at + pair] = jnp.where(
                    low, src[b, x, :, 0:pair], src[b, x, :, width - pair:width]
                )
            tabs[k][b] = own[b]
            return carry

        lax.fori_loop(0, bricks, one, 0)
        for r in range(rims):
            offer[k, r] = own[rim[0, r]]

    def send(k):
        for d in range(4):
            @pl.when(peers[d][0])
            def _():
                remote(k, d).start()

    def receive(k):
        for d in range(4):
            @pl.when(peers[d][0])
            def _():
                remote(k, d ^ 1).wait_recv()

    def finish_sends(k):
        for d in range(4):
            @pl.when(peers[d][0])
            def _():
                remote(k, d).wait_send()

    def build_weights(k):
        weight_copy(k).wait()

        def one(t, carry):
            a = t // 3
            base = pl.multiple_of((t - 3 * a) * ktile, ktile)
            for j in range(4):
                block = wbuf[k, t, j]
                hi = block.astype(jnp.bfloat16)
                lo = (block - hi.astype(jnp.float32)).astype(jnp.bfloat16)
                for q in range(2):
                    z = j - 1 + 2 * q
                    row = base + (z if z >= 0 else 5) * ch
                    row = pl.multiple_of(row, ch)
                    lanes = slice(q * pair, (q + 1) * pair)
                    whi[a, pl.ds(row, ch), lanes] = hi
                    whi[a, pl.ds(pl.multiple_of(row + kdy, ch), ch), lanes] = hi
                    wlo[a, pl.ds(row, ch), lanes] = lo
            return carry

        lax.fori_loop(0, 9, one, 0)

    def row_of(center, below, above, mask):
        return jnp.concatenate(
            [
                center[:, :half],
                jnp.where(mask, center[:, half:half + pair], below),
                center[:, half:],
                jnp.where(mask, above, center[:, half - pair:half]),
            ],
            axis=1,
        )

    def build_columns(src, k):
        tab = tabs[k]

        def one(b, carry):
            def entry(dx, dy, dz):
                return nbr[b, direction_number(dx, dy, dz)]

            for dx, xrow, s in ((-1, 0, 1), (1, SIDE + 1, 0)):
                pad[xrow, 1:SIDE + 1, :] = row_of(
                    tab[entry(dx, 0, 0), s],
                    tab[entry(dx, 0, -1), s, :, width - pair:width],
                    tab[entry(dx, 0, 1), s, :, 0:pair],
                    low,
                )
                for dy, yrow, y in ((-1, 0, SIDE - 1), (1, SIDE + 1, 0)):
                    pad[xrow, yrow:yrow + 1, :] = row_of(
                        tab[entry(dx, dy, 0), s, y:y + 1, :],
                        tab[entry(dx, dy, -1), s, y:y + 1, width - pair:width],
                        tab[entry(dx, dy, 1), s, y:y + 1, 0:pair],
                        low1,
                    )
            nlow, nhigh = entry(0, 0, -1), entry(0, 0, 1)
            for x in range(SIDE):
                at = (x % 4) * pair
                pad[1 + x, 1:SIDE + 1, :] = row_of(
                    src[b, x],
                    tab[nlow, 4 + x // 4, :, at:at + pair],
                    tab[nhigh, 4 + x // 4, :, at:at + pair],
                    low,
                )
            for dy, yrow, s in ((-1, 0, 3), (1, SIDE + 1, 2)):
                rows = row_of(
                    tab[entry(0, dy, 0), s],
                    tab[entry(0, dy, -1), s, :, width - pair:width],
                    tab[entry(0, dy, 1), s, :, 0:pair],
                    low,
                )
                for x in range(SIDE):
                    pad[1 + x, yrow:yrow + 1, :] = rows[x:x + 1]
            at = pl.multiple_of(b * 2 * SIDE, 2 * SIDE)
            for x in range(SIDE + 2):
                for dy in range(3):
                    v = pad[x, dy:dy + SIDE, :]
                    v = jnp.concatenate([v[:, :ktile], v[:, ktile:]], axis=0)
                    hi = v.astype(jnp.bfloat16)
                    lo = (v - hi.astype(jnp.float32)).astype(jnp.bfloat16)
                    cols[x, pl.ds(at, 2 * SIDE), dy * ktile:(dy + 1) * ktile] = hi
                    cols[x, pl.ds(at, 2 * SIDE), kdy + dy * ktile:kdy + (dy + 1) * ktile] = lo
            return carry

        lax.fori_loop(0, bricks, one, 0)

    def convolve():
        rows = SIDE * bricks * 2 * SIDE
        total = None
        for a in range(3):
            left = cols[a:a + SIDE].reshape(rows, 2 * kdy)
            term = jnp.dot(left, whi[a], preferred_element_type=jnp.float32)
            total = term if total is None else total + term
            left = cols[a:a + SIDE, :, :kdy].reshape(rows, kdy)
            total = total + jnp.dot(left, wlo[a], preferred_element_type=jnp.float32)
        acc[...] = total.reshape(acc.shape)

    def epilogue(k, res, dst):
        bvec = bias[k:k + 1, :]
        bvec = jnp.concatenate([bvec, bvec, bvec, bvec], axis=1)

        def one(b, carry):
            m = mask_of(b)
            for x in range(SIDE):
                for t in range(2):
                    at = pl.multiple_of(b * 2 * SIDE + t * SIDE, SIDE)
                    v = acc[x, pl.ds(at, SIDE), :] + bvec
                    lanes = slice(t * half, (t + 1) * half)
                    if res is not None:
                        v = v + res[b, x, :, lanes]
                    dst[b, x, :, lanes] = jnp.maximum(v, 0.0) * m
            return carry

        lax.fori_loop(0, bricks, one, 0)

    def mask_features(b, carry):
        cur[b] = feat[b] * mask_of(b)
        return carry

    lax.fori_loop(0, bricks, mask_features, 0)
    take_faces(cur, 0)
    arrivals = sum(jnp.where(has, 1, 0) for has, _ in peers)
    pl.semaphore_wait(barrier, arrivals)
    send(0)

    whi[...] = jnp.zeros_like(whi)
    wlo[...] = jnp.zeros_like(wlo)
    last = bricks + 4 * rims
    for k in range(convs):
        tabs[k][last] = jnp.zeros(tabs[k].shape[1:], jnp.float32)
    for d in range(4):
        @pl.when(jnp.logical_not(peers[d][0]))
        def _():
            for k in range(convs):
                for r in range(rims):
                    tabs[k][bricks + rims * d + r] = jnp.zeros(tabs[k].shape[1:], jnp.float32)

    for k in range(convs):
        src = cur if k % 2 == 0 else hid
        if k % 2 == 0:
            dst = hid
        else:
            dst = cur if k < convs - 1 else out
        build_weights(k)
        receive(k)
        build_columns(src, k)
        convolve()
        epilogue(k, None if k % 2 == 0 else cur, dst)
        if k < convs - 1:
            take_faces(dst, k + 1)
            send(k + 1)
    for k in range(convs):
        finish_sends(k)


def shards(nsp, nsl, features, live, rim_slots, neighbours, weights, biases):
    bricks, _, _, width = features.shape
    ch = biases.shape[-1]
    convs = weights.shape[0]
    rims = rim_slots.shape[-1]
    entries = bricks + 4 * rims + 1
    taps = weights.reshape(convs, 9, 3, ch, ch)
    none = jnp.zeros((convs, 9, 1, ch, ch), jnp.float32)
    blocks = jnp.concatenate(
        [jnp.concatenate([taps, none], 2), jnp.concatenate([none, taps], 2)], -1
    )
    half = width // 2
    kdy = 3 * (half + 2 * ch)
    f32, bf16 = jnp.float32, jnp.bfloat16
    smem = pl.BlockSpec(memory_space=pltpu.SMEM)
    vmem = pl.BlockSpec(memory_space=pltpu.VMEM)
    return pl.pallas_call(
        functools.partial(layers_kernel, nsp, nsl),
        out_shape=jax.ShapeDtypeStruct(features.shape, f32),
        in_specs=[smem, smem, smem, vmem, vmem, pl.BlockSpec(memory_space=pl.ANY)],
        out_specs=vmem,
        scratch_shapes=[
            pltpu.VMEM(features.shape, f32),
            pltpu.VMEM(features.shape, f32),
            pltpu.VMEM((bricks, 6, SIDE, width), f32),
            pltpu.VMEM((convs, rims, 6, SIDE, width), f32),
            pltpu.VMEM((SIDE + 2, 2 * SIDE, width + 4 * ch), f32),
            pltpu.VMEM((SIDE + 2, bricks * 2 * SIDE, 2 * kdy), bf16),
            pltpu.VMEM((3, 2 * kdy, half), bf16),
            pltpu.VMEM((3, kdy, half), bf16),
            pltpu.VMEM((convs, 9, 4, ch, 2 * ch), f32),
            pltpu.VMEM((SIDE, bricks * 2 * SIDE, half), f32),
            pltpu.SemaphoreType.DMA((convs,)),
            pltpu.SemaphoreType.DMA((convs, 4)),
            pltpu.SemaphoreType.DMA((convs, 4)),
        ]
        + [pltpu.VMEM((entries, 6, SIDE, width), f32) for _ in range(convs)],
        compiler_params=pltpu.CompilerParams(
            collective_id=0, has_side_effects=True, vmem_limit_bytes=56 * 1024 * 1024
        ),
        name="layers",
    )(neighbours, live, rim_slots, features, biases, blocks)


def solution(mesh):
    in_specs = (
        P(("space", "slab"), None, None, None),
        P(("space", "slab")),
        P(("space", "slab"), None),
        P(("space", "slab"), None),
        P(),
        P(),
    )
    out_specs = P(("space", "slab"), None, None, None)
    body = functools.partial(shards, mesh.shape["space"], mesh.shape["slab"])
    return jax.shard_map(body, mesh=mesh, in_specs=in_specs, out_specs=out_specs, check_vma=False)
```

profile of v0, /device:TPU:12, one launch (start us, length us, event | category | flops | bytes accessed | tf_op | source)
XLA Modules:
  0.0 77.2 jit_solution(10629643830169525451)
XLA Ops:
  0.0 3.1 %reshape.3 = f32[4,9,3,64,64]{4,3,0,2,1:T(8,128)S(1)} reshape(f32[4,27,4096]{2,0,1:T(4,128)} %param.10) | data formatting | bytes 3538944 | tf_op jit(solution)/shard_map/reshape | solution.py:268
  3.1 3.2 %select_maximum_fusion.w_hbm = f32[4,9,4,64,128]{4,3,2,1,0:T(8,128)} fusion(f32[4,9,3,64,64]{4,3,0,2,1:T(8,128)S(1)} %reshape.3), kind=kLoop, calls=%fused_computation | loop fusion | flops 5898240 | bytes 6488064 | tf_op jit(solution)/shard_map/concatenate | solution.py:270
  7.0 68.3 %layers.1 = f32[4,8,8,512]{3,2,1,0:T(8,128)} custom-call(s32[4,26]{1,0:T(4,128)} %nbr.1, s32[1]{0:T(128)S(6)} %copy.13.live, s32[1,2]{1,0:T(1,128)} %rim.1, f32[4,8,8,512]{3,2,1,0:T(8,128)} %feat.1, f32[4,64]{1,0:T(4,128)} %bias.1, f32[4,9,4,64,128]{4,3,2,1,0:T(8,128)} %select_maximum_fusion.w_hbm), custom_call_target="tpu_custom_call" | custom-call | tf_op jit(solution)/shard_map/layers/pallas_call | solution.py:278
  75.3 1.9 %copy.14 = f32[4,8,8,512]{3,2,1,0:T(8,128)} copy(f32[4,8,8,512]{3,2,1,0:T(8,128)} %layers.1) | data formatting | bytes 1048576
where the time goes:
time: 77.4 us; the launch traced here: 77.2 us
  Pallas kernels  68.3 us (88%)
  local copies, waits for them, and re-layouts  4.95 us (6%)
  other arithmetic  3.21 us (4%)
    pallas_call x1, Pallas kernels, shards(): pl.pallas_call(functools.partial(layers_kernel, nsp, nsl), out_shape=jax....  68.3 us
    concatenate x1, other arithmetic, shards(): jnp.concatenate([jnp.concatenate([taps, none], 2), jnp.concatenate([none,...  3.21 us
    reshape x1, local copies, waits for them, and re-layouts, shards(): taps = weights.reshape(convs, 9, 3, ch, ch)  3.08 us
    unnamed x1, local copies, waits for them, and re-layouts  1.87 us

commit v1 on v0

--- a/solution.py
+++ b/solution.py
@@ -29,7 +29,7 @@
     ktile = half + pair
     kdy = 3 * ktile
     rims = offer.shape[1]
-    convs = w_hbm.shape[0]
+    convs = w_hbm.shape[1]
     sp = lax.axis_index("space")
     sl = lax.axis_index("slab")
     peers = (
@@ -46,7 +46,7 @@
             pl.semaphore_signal(barrier, inc=1, device_id=peer, device_id_type=MESH)
 
     def weight_copy(k):
-        return pltpu.make_async_copy(w_hbm.at[k], wbuf.at[k], wsem.at[k])
+        return pltpu.make_async_copy(w_hbm.at[:, k], wbuf.at[k], wsem.at[k])
 
     for k in range(convs):
         weight_copy(k).start()
@@ -111,8 +111,12 @@
         def one(t, carry):
             a = t // 3
             base = pl.multiple_of((t - 3 * a) * ktile, ktile)
+            taps = [wbuf[k, 3 * t + i] for i in range(3)]
+            none = jnp.zeros((ch, ch), jnp.float32)
             for j in range(4):
-                block = wbuf[k, t, j]
+                block = jnp.concatenate(
+                    [taps[j] if j < 3 else none, taps[j - 1] if j > 0 else none], axis=1
+                )
                 hi = block.astype(jnp.bfloat16)
                 lo = (block - hi.astype(jnp.float32)).astype(jnp.bfloat16)
                 for q in range(2):
@@ -265,11 +269,7 @@
     convs = weights.shape[0]
     rims = rim_slots.shape[-1]
     entries = bricks + 4 * rims + 1
-    taps = weights.reshape(convs, 9, 3, ch, ch)
-    none = jnp.zeros((convs, 9, 1, ch, ch), jnp.float32)
-    blocks = jnp.concatenate(
-        [jnp.concatenate([taps, none], 2), jnp.concatenate([none, taps], 2)], -1
-    )
+    taps = weights.transpose(1, 0, 2).reshape(weights.shape[1], convs, ch, ch)
     half = width // 2
     kdy = 3 * (half + 2 * ch)
     f32, bf16 = jnp.float32, jnp.bfloat16
@@ -289,7 +289,7 @@
             pltpu.VMEM((SIDE + 2, bricks * 2 * SIDE, 2 * kdy), bf16),
             pltpu.VMEM((3, 2 * kdy, half), bf16),
             pltpu.VMEM((3, kdy, half), bf16),
-            pltpu.VMEM((convs, 9, 4, ch, 2 * ch), f32),
+            pltpu.VMEM((convs, weights.shape[1], ch, ch), f32),
             pltpu.VMEM((SIDE, bricks * 2 * SIDE, half), f32),
             pltpu.SemaphoreType.DMA((convs,)),
             pltpu.SemaphoreType.DMA((convs, 4)),
@@ -300,7 +300,7 @@
             collective_id=0, has_side_effects=True, vmem_limit_bytes=56 * 1024 * 1024
         ),
         name="layers",
-    )(neighbours, live, rim_slots, features, biases, blocks)
+    )(neighbours, live, rim_slots, features, biases, taps)
 
 
 def solution(mesh):

time: 77.4 us -> 75.2 us (0.972)
  other arithmetic: 3.21 us -> 0 us
  local copies, waits for them, and re-layouts: 4.95 us -> 6.04 us
    concatenate x1 -> x0, other arithmetic: 3.21 us -> none  [shards(): jnp.concatenate([jnp.concatenate([taps, none], 2), jnp.concatenate([none,...]
    reshape x1, local copies, waits for them, and re-layouts: 3.08 us -> 4.18 us  [shards(): taps = weights.transpose(1, 0, 2).reshape(weights.shape[1], convs, ch, ch)]
where the time goes in v1:
time: 75.2 us; the launch traced here: 75 us
  Pallas kernels  68.3 us (91%)
  local copies, waits for them, and re-layouts  6.04 us (8%)
    pallas_call x1, Pallas kernels, shards(): pl.pallas_call(functools.partial(layers_kernel, nsp, nsl), out_shape=jax....  68.3 us
    reshape x1, local copies, waits for them, and re-layouts, shards(): taps = weights.transpose(1, 0, 2).reshape(weights.shape[1], convs, ch, ch)  4.18 us
    unnamed x1, local copies, waits for them, and re-layouts  1.87 us

profile of v1, /device:TPU:12, one launch (start us, length us, event | category | flops | bytes accessed | tf_op | source)
XLA Modules:
  0.0 75.0 jit_solution(16795077434405720776)
XLA Ops:
  0.7 4.2 %reshape.3.w_hbm = f32[27,4,64,64]{3,2,1,0:T(8,128)} reshape(f32[27,4,4096]{2,1,0:T(4,128)} %bitcast.1) | data formatting | bytes 3538944 | tf_op jit(solution)/shard_map/reshape | solution.py:272
  4.8 68.3 %layers.1 = f32[4,8,8,512]{3,2,1,0:T(8,128)} custom-call(s32[4,26]{1,0:T(4,128)} %nbr.1, s32[1]{0:T(128)S(6)} %copy.8.live, s32[1,2]{1,0:T(1,128)} %rim.1, f32[4,8,8,512]{3,2,1,0:T(8,128)} %feat.1, f32[4,64]{1,0:T(4,128)} %bias.1, f32[27,4,64,64]{3,2,1,0:T(8,128)} %reshape.3.w_hbm), custom_call_target="tpu_custom_call" | custom-call | tf_op jit(solution)/shard_map/layers/pallas_call | solution.py:278
  73.1 1.9 %copy.9 = f32[4,8,8,512]{3,2,1,0:T(8,128)} copy(f32[4,8,8,512]{3,2,1,0:T(8,128)} %layers.1) | data formatting | bytes 1048576
